TPU v7x, 512 devices: a whole 4x4x16 slice. The times are simulated.
512 devices in a mesh: dp: 2 (over z_hi), fsdp: 16 (over z_lo, core), tile: 16 (over y, x).
Axes of the slice: x: 4, y: 4, z: 16 (z_hi: 2, z_lo: 8; z = z_hi * 8 + z_lo), core: 2. Of those that a mesh axis runs over, the one named last changes fastest.
Arguments:
- tokens: bfloat16 [32, 8, 512, 1536], P(('dp', 'fsdp'), None, 'tile'), may hold values from -6 to 6
- norm_gain: float32 [1536], replicated, may hold values from 0.25 to 1.75
- query_key_value_weight: bfloat16 [1536, 2304], P('fsdp'), may hold values from -5 to 5
- out_weight: bfloat16 [768, 1536], P('fsdp'), may hold values from -0.21875 to 0.21875
- head_weight: bfloat16 [1536, 320], P('fsdp'), may hold values from -0.15625 to 0.15625
- coarse: float32 [32, 20, 8, 512], P(('dp', 'fsdp'), None, None, 'tile'), may hold values from -36 to 36
- grad_fine: float32 [32, 20, 32, 2048], P(('dp', 'fsdp'), None, None, 'tile'), may hold values from -0.6 to 0.6
Outputs:
- fine_grid: float32 [32, 20, 32, 2048], P(('dp', 'fsdp'), None, None, 'tile')
- grad_tokens: bfloat16 [32, 8, 512, 1536], P(('dp', 'fsdp'), None, 'tile')
- grad_head: float32 [1536, 320], P('fsdp')
All inputs are finite; a program needn't handle non-finite values.
Results may differ from a plain program's by a relative error of at most 0.0059.
Values may be sent and summed in bfloat16 or wider, within the bound.
No kernel may reach another device: no remote copies, remote signals or barrier semaphores. Data moves between devices by JAX's collectives and lax.ppermute only.
A program may use at most 64 MiB of HBM per device.

v0:
```python
import jax
import jax.numpy as jnp
from jax import lax
from jax.sharding import PartitionSpec as P

D = 1536
HEADS = 8
HEAD_DIM = 96
VARS = 20
MARGIN = 8
INNER = 768
HEAD_OUT = 320
EPSILON = 1e-05


def with_halo(shard, sides, width):
    for axis, dim in sides:
        devices, length = (lax.axis_size(axis), shard.shape[dim])
        up = [(i, (i + 1) % devices) for i in range(devices)]
        down = [(j, i) for i, j in up]
        last = lax.slice_in_dim(shard, length - width, length, axis=dim)
        leading = lax.slice_in_dim(shard, 0, width, axis=dim)
        before = lax.ppermute(last, axis, up)
        after = lax.ppermute(leading, axis, down)
        shard = jnp.concatenate([before, shard, after], axis=dim)
    return shard


def from_behind(value, axis, steps):
    count = lax.axis_size(axis)
    pairs = [(source, (source + steps) % count) for source in range(count)]
    return lax.ppermute(value, axis, pairs)


def layer_norm(values):
    average = jnp.mean(values, axis=-1, keepdims=True)
    centred = values - average
    variance = jnp.mean(centred * centred, axis=-1, keepdims=True)
    inverse_dev = lax.rsqrt(variance + EPSILON)
    return (centred * inverse_dev, inverse_dev)


def norm_backward(grad_normed, standard, inverse_dev, norm_gain):
    grad_standard = grad_normed * norm_gain
    first_mean = jnp.mean(grad_standard, axis=-1, keepdims=True)
    second_mean = jnp.mean(grad_standard * standard, axis=-1, keepdims=True)
    return inverse_dev * (grad_standard - first_mean - standard * second_mean)


def attend_forward(queries, keys_values):
    query_count = queries.shape[0]
    key_count = keys_values.shape[0]
    score_scale = HEAD_DIM ** (-0.5)
    query_heads = queries.reshape(query_count, HEADS, HEAD_DIM)
    key_heads = keys_values[:, :INNER].reshape(key_count, HEADS, HEAD_DIM)
    value_heads = keys_values[:, INNER:].reshape(key_count, HEADS, HEAD_DIM)
    scores = (
        jnp.einsum("qhd,khd->hqk", query_heads, key_heads, preferred_element_type=jnp.float32)
        * score_scale
    )
    biggest = jnp.max(scores, axis=-1, keepdims=True)
    exponent = jnp.exp(scores - biggest)
    softmax_out = exponent / jnp.sum(exponent, axis=-1, keepdims=True)
    softmax_low = softmax_out.astype(jnp.bfloat16)
    attended = jnp.einsum(
        "hqk,khd->qhd", softmax_low, value_heads, preferred_element_type=jnp.float32
    )
    return (attended.astype(jnp.bfloat16).reshape(query_count, INNER), softmax_out)


def attend_backward(softmax_out, queries, keys_values, grad_attended):
    query_count = queries.shape[0]
    key_count = keys_values.shape[0]
    score_scale = HEAD_DIM ** (-0.5)
    query_heads = queries.reshape(query_count, HEADS, HEAD_DIM)
    key_heads = keys_values[:, :INNER].reshape(key_count, HEADS, HEAD_DIM)
    value_heads = keys_values[:, INNER:].reshape(key_count, HEADS, HEAD_DIM)
    grad_heads = grad_attended.reshape(query_count, HEADS, HEAD_DIM)
    softmax_low = softmax_out.astype(jnp.bfloat16)
    grad_values = jnp.einsum(
        "hqk,qhd->khd", softmax_low, grad_heads, preferred_element_type=jnp.float32
    )
    grad_weights = jnp.einsum(
        "qhd,khd->hqk", grad_heads, value_heads, preferred_element_type=jnp.float32
    )
    weighted = jnp.sum(softmax_out * grad_weights, axis=-1, keepdims=True)
    grad_scores = (softmax_out * (grad_weights - weighted)).astype(jnp.bfloat16)
    grad_queries = (
        jnp.einsum("hqk,khd->qhd", grad_scores, key_heads, preferred_element_type=jnp.float32)
        * score_scale
    )
    grad_keys = (
        jnp.einsum("hqk,qhd->khd", grad_scores, query_heads, preferred_element_type=jnp.float32)
        * score_scale
    )
    pair_gradient_rows = jnp.concatenate(
        [grad_keys.reshape(key_count, INNER), grad_values.reshape(key_count, INNER)], axis=1
    )
    return (grad_queries.astype(jnp.bfloat16).reshape(query_count, INNER), pair_gradient_rows)


def interp_weights(fine_index):
    coarse_cell = fine_index // 4
    phase_index = fine_index % 4
    lower_shift = (phase_index < 2).astype(jnp.int32)
    upper_weight = (2 * phase_index - 3 + 8 * lower_shift).astype(jnp.float32) / 8.0
    return (coarse_cell - lower_shift, upper_weight)


def build_matrix(lower_cell, upper_cell, upper_weight, count):
    columns = jnp.arange(count, dtype=jnp.int32)
    lower_part = jnp.where(
        columns[None, :] == lower_cell[:, None], 1.0 - upper_weight[:, None], 0.0
    )
    upper_portion = jnp.where(columns[None, :] == upper_cell[:, None], upper_weight[:, None], 0.0)
    return lower_part + upper_portion


def contract_last(left_side, right_side):
    return lax.dot_general(
        left_side, right_side, (((1,), (1,)), ((), ())), preferred_element_type=jnp.float32
    )


def shards(tokens, norm_gain, query_key_value_weight, out_weight, head_weight, coarse, grad_fine):
    lat_rows = tokens.shape[1]
    lon_cols = tokens.shape[2]
    row_count = lat_rows * lon_cols
    flattened_rows = tokens[0].reshape(row_count, D).astype(jnp.float32)
    standard, inverse_dev = layer_norm(flattened_rows)
    normed = (standard * norm_gain).astype(jnp.bfloat16)
    full_qkv = lax.all_gather(query_key_value_weight, "fsdp", axis=0, tiled=True)
    projected = jnp.dot(normed, full_qkv, preferred_element_type=jnp.float32).astype(jnp.bfloat16)
    queries = projected[:, :INNER]
    pairs_local = projected[:, INNER:]
    margin_pairs = with_halo(
        pairs_local.reshape(lat_rows, lon_cols, 2 * INNER), (("tile", 1),), MARGIN
    )
    keys_values = margin_pairs.reshape(lat_rows * (lon_cols + 2 * MARGIN), 2 * INNER)
    attended, softmax_out = attend_forward(queries, keys_values)
    full_out = lax.all_gather(out_weight, "fsdp", axis=0, tiled=True)
    mixed_out = jnp.dot(attended, full_out, preferred_element_type=jnp.float32)
    hidden = (flattened_rows + mixed_out).astype(jnp.bfloat16)
    full_head = lax.all_gather(head_weight, "fsdp", axis=0, tiled=True)
    head_out = jnp.dot(hidden, full_head, preferred_element_type=jnp.float32)
    fine_head = (
        head_out.reshape(lat_rows, lon_cols, VARS, 4, 4)
        .transpose(2, 0, 3, 1, 4)
        .reshape(VARS, 4 * lat_rows, 4 * lon_cols)
    )
    coarse_padded_grid = with_halo(coarse[0], (("tile", 2),), 1)
    lat_lower, lat_upper_weight = interp_weights(jnp.arange(4 * lat_rows, dtype=jnp.int32))
    latitude_matrix = build_matrix(
        jnp.clip(lat_lower, 0, lat_rows - 1),
        jnp.clip(lat_lower + 1, 0, lat_rows - 1),
        lat_upper_weight,
        lat_rows,
    )
    lon_lower, lon_upper_weight = interp_weights(jnp.arange(4 * lon_cols, dtype=jnp.int32))
    lon_matrix = build_matrix(lon_lower + 1, lon_lower + 2, lon_upper_weight, lon_cols + 2)
    incomplete_grid = jnp.einsum(
        "lj,kji->kli", latitude_matrix, coarse_padded_grid, precision=lax.Precision.HIGHEST
    )
    residual = jnp.einsum(
        "vrb,cb->vrc", incomplete_grid, lon_matrix, precision=lax.Precision.HIGHEST
    )
    fine_grid = fine_head + residual
    grad_rows = (
        grad_fine[0]
        .reshape(VARS, lat_rows, 4, lon_cols, 4)
        .transpose(1, 3, 0, 2, 4)
        .reshape(row_count, HEAD_OUT)
    )
    grad_rows = grad_rows.astype(jnp.bfloat16)
    head_term = lax.dot_general(
        hidden, grad_rows, (((0,), (0,)), ((), ())), preferred_element_type=jnp.float32
    )
    head_block = lax.psum_scatter(head_term, "fsdp", scatter_dimension=0, tiled=True)
    grad_head = lax.psum(head_block, ("dp", "tile"))
    grad_hidden = contract_last(grad_rows, full_head)
    grad_attended = contract_last(grad_hidden.astype(jnp.bfloat16), full_out).astype(jnp.bfloat16)
    grad_queries, pair_gradient_rows = attend_backward(
        softmax_out, queries, keys_values, grad_attended
    )
    pair_gradient_rows = pair_gradient_rows.reshape(lat_rows, lon_cols + 2 * MARGIN, 2 * INNER)
    from_left = from_behind(pair_gradient_rows[:, lon_cols + MARGIN :], "tile", 1)
    from_right = from_behind(pair_gradient_rows[:, :MARGIN], "tile", -1)
    own_cells = pair_gradient_rows[:, MARGIN : MARGIN + lon_cols]
    own_cells = own_cells + jnp.pad(from_left, ((0, 0), (0, lon_cols - MARGIN), (0, 0)))
    own_cells = own_cells + jnp.pad(from_right, ((0, 0), (lon_cols - MARGIN, 0), (0, 0)))
    grad_all = jnp.concatenate(
        [grad_queries, own_cells.reshape(row_count, 2 * INNER).astype(jnp.bfloat16)], axis=1
    )
    grad_normed = contract_last(grad_all, full_qkv)
    grad_input = grad_hidden + norm_backward(grad_normed, standard, inverse_dev, norm_gain)
    grad_tokens = grad_input.astype(jnp.bfloat16).reshape(1, lat_rows, lon_cols, D)
    return (fine_grid[None], grad_tokens, grad_head)


def solution(mesh):
    placed = (
        P(("dp", "fsdp"), None, "tile", None),
        P(),
        P("fsdp", None),
        P("fsdp", None),
        P("fsdp", None),
        P(("dp", "fsdp"), None, None, "tile"),
        P(("dp", "fsdp"), None, None, "tile"),
    )
    return jax.shard_map(
        shards,
        mesh=mesh,
        in_specs=placed,
        out_specs=(
            P(("dp", "fsdp"), None, None, "tile"),
            P(("dp", "fsdp"), None, "tile", None),
            P("fsdp", None),
        ),
        check_vma=False,
    )
```

profile of v0, /device:TPU:2, one launch (start us, length us, event | category | flops | bytes accessed | tf_op | source)
XLA Modules:
  0.0 943.6 jit_solution(4857148850893295786)
XLA Ops:
  7.2 0.7 all-gather.3.cloned.1.call-update
  8.0 0.7 all-gather.5.cloned.1.call-update
  8.7 1.7 fusion.56
  10.4 3.4 collective-permute-start.2
  13.8 6.3 collective-permute-start.3
  20.1 1.3 convert_reduce_fusion
  22.0 0.5 copy.22
  22.5 1.5 copy.23
  24.0 1.1 convert_element_type.125
  25.1 0.6 broadcast_add_fusion
  25.7 46.6 %all_gather.11 = bf16[1536,320]{1,0:T(8,128)(2,1)S(1)} all-gather(bf16[96,320]{1,0:T(8,128)(2,1)} %param.11), channel_id=1, replica_groups=mesh['dp'=2,'fsdp'=16,'tile'=16] {'fsdp'}, dimensions={0}, use_global_device_ids=true | all-gather | bytes 1044480 | tf_op jit(solution)/shard_map/all_gather | solution.py:144
  72.3 1.6 fusion.59
  73.9 1.2 multiply_convert_fusion.1
  75.1 0.6 convert_multiply_fusion
  75.7 2.1 convolution_bitcast_fusion.1
  77.8 55.1 %all-gather.3.cloned.1.call-done = bf16[1536,2304]{1,0:T(8,128)(2,1)} async-done(((bf16[96,2304]{1,0:T(8,128)(2,1)}), bf16[1536,2304]{1,0:T(8,128)(2,1)}) %all-gather.3.cloned.1.call-update) | async-done | bytes 7077904 | tf_op jit(solution)/shard_map/all_gather | solution.py:132
  132.9 5.3 convolution_convert_fusion
  138.2 0.9 copy-done.7
  139.2 0.8 fusion.55
  140.0 3.2 collective-permute-start
  143.2 2.8 collective-permute-start.1
  146.0 86.6 %all-gather.5.cloned.1.call-done = bf16[768,1536]{1,0:T(8,128)(2,1)} async-done(((bf16[48,1536]{1,0:T(8,128)(2,1)}), bf16[768,1536]{1,0:T(8,128)(2,1)}) %all-gather.5.cloned.1.call-update) | async-done | bytes 2359312 | tf_op jit(solution)/shard_map/all_gather | solution.py:141
  232.6 3.2 convolution_convert_fusion.1
  235.8 1.9 copy.24
  237.8 1.8 slice.50
  239.6 1.9 copy.18
  241.5 1.4 pad_maximum_fusion
  242.9 1.1 fusion.54
  243.9 2.1 copy.29
  246.1 2.1 copy.28
  248.2 4.0 fusion.57
  252.2 2.9 convolution_convert_fusion.2
  255.2 0.8 fusion.4
  256.0 1.3 fusion.58
  257.3 2.0 fusion.60
  259.3 1.4 reshape.187
  260.7 3.0 copy.20
  263.8 3.0 copy.21
  266.8 2.6 convolution_bitcast_fusion
  269.3 1.6 copy.26
  271.0 2.7 concatenate.20
  273.8 1.0 copy-done.16
  274.9 3.0 multiply_reduce_fusion
  277.9 0.7 multiply_convert_fusion
  278.6 1.1 copy-done.1
  279.8 0.4 fusion.9
  280.2 1.7 copy.25
  281.9 1.9 concatenate.19
  283.9 1.1 copy-done.8
  285.2 1.5 copy-done.5
  286.7 1.0 fusion.53
  287.6 3.4 collective-permute-start.4
  291.1 2.8 collective-permute-start.5
  293.9 0.6 fusion.10
  294.5 1.0 copy.27
  295.5 1.1 fusion.11
  296.7 3.5 collective-permute-done.4
  300.2 3.3 collective-permute-done.5
  303.5 1.7 fusion.6
  305.2 6.3 fusion.52
  311.6 73.0 %reduce-scatter.2.cloned.1.call-done = f32[96,320]{1,0:T(8,128)} async-done(((f32[1536,320]{1,0:T(8,128)}), f32[96,320]{1,0:T(8,128)}) %reduce-scatter.2.cloned.1.call-update) | async-done | bytes 122896 | tf_op jit(solution)/shard_map/reduce_scatter | solution.py:178
  384.5 2.9 add_convert_fusion
  387.4 548.1 %all-reduce.4.cloned.1.call-done = f32[96,320]{1,0:T(8,128)} async-done(((f32[96,320]{1,0:T(8,128)}), f32[96,320]{1,0:T(8,128)}) %all-reduce.4.cloned.1.call-update) | async-done | bytes 122896 | tf_op jit(solution)/shard_map/psum | solution.py:179
  935.5 1.6 copy.32
  (69 shorter events, 1.3 us)
Async XLA Ops:
  7.2 14.4 %copy-start = (bf16[1,8,32,1536]{3,2,1,0:T(8,128)(2,1)S(1)}, bf16[1,8,32,1536]{3,2,1,0:T(8,128)(2,1)}, u32[]{:S(2)}) copy-start(bf16[1,8,32,1536]{3,2,1,0:T(8,128)(2,1)} %param.7) | copy-start | bytes 2359300
  7.2 14.8 %copy-start.19 = (f32[1,20,32,128]{3,2,1,0:T(8,128)S(1)}, f32[1,20,32,128]{3,2,1,0:T(8,128)}, u32[]{:S(2)}) copy-start(f32[1,20,32,128]{3,2,1,0:T(8,128)} %param.13) | copy-start | bytes 983044
  7.2 125.7 %all-gather.3.cloned.1.call-start = ((), (), s32[]{:S(2)}) async-start(), calls=%async_computation.1 | async-start | bytes 7520256 | tf_op jit(solution)/shard_map/all_gather | solution.py:132
  7.9 224.7 %all-gather.5.cloned.1.call-start = ((), (), s32[]{:S(2)}) async-start(), calls=%async_computation.2 | async-start | bytes 2506752 | tf_op jit(solution)/shard_map/all_gather | solution.py:141
  8.7 375.8 %reduce-scatter.2.cloned.1.call-start = ((), (), s32[]{:S(2)}) async-start(), calls=%async_computation.3 | async-start | bytes 2506752 | tf_op jit(solution)/shard_map/reduce_scatter | solution.py:178
  10.4 65.2 %collective-permute-start.2 = (f32[20,8,1]{2,1,0:T(8,128)}, f32[20,8,1]{2,1,0:T(8,128)}, u32[]{:S(2)}, u32[]{:S(2)}) collective-permute-start(f32[20,8,1]{2,1,0:T(8,128)} %get-tuple-element.11), channel_id=1, source_target_pairs={{0,1},{1,2},{2,3},{3,4},{4,5},{5,6},{6,7},{7,8},{8,9},{9,10},{10,1... | collective-permute-start | bytes 1928 | tf_op jit(solution)/shard_map/ppermute | solution.py:23
  13.8 61.8 %collective-permute-start.3 = (f32[20,8,1]{2,1,0:T(8,128)}, f32[20,8,1]{2,1,0:T(8,128)}, u32[]{:S(2)}, u32[]{:S(2)}) collective-permute-start(f32[20,8,1]{2,1,0:T(8,128)} %get-tuple-element.12), channel_id=1, source_target_pairs={{1,0},{2,1},{3,2},{4,3},{5,4},{6,5},{7,6},{8,7},{9,8},{10,9},{11,1... | collective-permute-start | bytes 1928 | tf_op jit(solution)/shard_map/ppermute | solution.py:24
  72.3 1.6 copy-start.20
  72.3 3.4 copy-start.15
  138.2 1.8 copy-start.14
  138.2 1.0 copy-start.7
  140.0 101.5 %collective-permute-start = (bf16[8,8,1536]{2,1,0:T(8,128)(2,1)}, bf16[8,8,1536]{2,1,0:T(8,128)(2,1)}, u32[]{:S(2)}, u32[]{:S(2)}) collective-permute-start(bf16[8,8,1536]{2,1,0:T(8,128)(2,1)} %get-tuple-element.9), channel_id=1, source_target_pairs={{0,1},{1,2},{2,3},{3,4},{4,5},{5,6},{6,7},{7,8},{8,9},{9,10},{10,1... | collective-permute-start | bytes 589832 | tf_op jit(solution)/shard_map/ppermute | solution.py:23
  143.2 98.3 %collective-permute-start.1 = (bf16[8,8,1536]{2,1,0:T(8,128)(2,1)}, bf16[8,8,1536]{2,1,0:T(8,128)(2,1)}, u32[]{:S(2)}, u32[]{:S(2)}) collective-permute-start(bf16[8,8,1536]{2,1,0:T(8,128)(2,1)} %get-tuple-element.10), channel_id=1, source_target_pairs={{1,0},{2,1},{3,2},{4,3},{5,4},{6,5},{7,6},{8,7},{9,8},{10,9},{11,1... | collective-permute-start | bytes 589832 | tf_op jit(solution)/shard_map/ppermute | solution.py:24
  252.2 2.9 copy-start.4
  256.0 1.3 copy-start.10
  257.3 2.0 copy-start.12
  273.7 1.1 copy-start.16
  273.7 1.2 copy-start.17
  273.7 661.8 %all-reduce.4.cloned.1.call-start = ((), (), s32[]{:S(2)}) async-start(), calls=%async_computation.4 | async-start | bytes 294912 | tf_op jit(solution)/shard_map/psum | solution.py:179
  274.9 3.0 copy-start.3
  277.9 1.9 copy-start.9
  278.6 1.2 copy-start.1
  283.8 1.3 copy-start.8
  285.0 8.9 copy-start.2
  285.0 8.9 copy-start.6
  285.2 1.5 copy-start.5
  287.6 12.6 %collective-permute-start.4 = (f32[8,8,1536]{2,1,0:T(8,128)}, f32[8,8,1536]{2,1,0:T(8,128)}, u32[]{:S(2)}, u32[]{:S(2)}) collective-permute-start(f32[8,8,1536]{2,1,0:T(8,128)} %get-tuple-element.5), channel_id=1, source_target_pairs={{0,1},{1,2},{2,3},{3,4},{4,5},{5,6},{6,7},{7,8},{8,9},{9,10},{10,1... | collective-permute-start | bytes 1179656 | tf_op jit(solution)/shard_map/ppermute | solution.py:32
  291.0 4.5 copy-start.11
  291.0 4.5 copy-start.13
  291.0 4.5 copy-start.22
  291.0 4.5 copy-start.23
  291.0 4.5 copy-start.24
  291.1 4.5 copy-start.25
  291.1 12.4 %collective-permute-start.5 = (f32[8,8,1536]{2,1,0:T(8,128)}, f32[8,8,1536]{2,1,0:T(8,128)}, u32[]{:S(2)}, u32[]{:S(2)}) collective-permute-start(f32[8,8,1536]{2,1,0:T(8,128)} %get-tuple-element.6), channel_id=1, source_target_pairs={{0,15},{1,0},{2,1},{3,2},{4,3},{5,4},{6,5},{7,6},{8,7},{9,8},{10,9... | collective-permute-start | bytes 1179656 | tf_op jit(solution)/shard_map/ppermute | solution.py:32
  296.7 8.5 copy-start.18
  296.7 8.6 copy-start.21
Sparse Core Ops, SparseCore 0:
  10.1 122.7 all-gather.2
  135.0 97.5 all-gather.4
  273.8 110.6 reduce-scatter.1
  387.3 548.2 all-reduce.3
where the time goes:
time: 945 us; the launch traced here: 944 us
  waiting for transfers between devices  771 us (82%)
  blocking collectives  46.6 us (5%)
  local copies, waits for them, and re-layouts  41.8 us (4%)
  matrix products  37.3 us (4%)
  starting transfers between devices  22.1 us (2%)
  between operations  14.2 us (2%)
  other arithmetic  10.8 us (1%)
    psum x1, waiting for transfers between devices, shards(): grad_head = lax.psum(head_block, ('dp', 'tile'))  548 us
    all_gather x1, waiting for transfers between devices, shards(): full_out = lax.all_gather(out_weight, 'fsdp', axis=0, tiled=True)  86.6 us
    reduce_scatter x1, waiting for transfers between devices, shards(): lax.psum_scatter(head_term, 'fsdp', scatter_dimension=0, tiled=True)  73 us
    all_gather x1, waiting for transfers between devices, shards(): lax.all_gather(query_key_value_weight, 'fsdp', axis=0, tiled=True)  55.1 us
    all_gather x1, blocking collectives, shards(): full_head = lax.all_gather(head_weight, 'fsdp', axis=0, tiled=True)  46.6 us
  transfers between devices with their start and end apart: 10, of which 6 were waited for; matrix products, arithmetic and copies ran while one was open for 5% of the time, Pallas kernels for 0%

commit v1 on v0

--- a/solution.py
+++ b/solution.py
@@ -176,7 +176,10 @@
         hidden, grad_rows, (((0,), (0,)), ((), ())), preferred_element_type=jnp.float32
     )
     head_block = lax.psum_scatter(head_term, "fsdp", scatter_dimension=0, tiled=True)
-    grad_head = lax.psum(head_block, ("dp", "tile"))
+    detail_domain_for = lambda piece_in, shard_axis, axis_name: lax.psum(
+        lax.psum(piece_in, shard_axis), axis_name
+    )
+    grad_head = detail_domain_for(head_block, "tile", axis_name="dp")
     grad_hidden = contract_last(grad_rows, full_head)
     grad_attended = contract_last(grad_hidden.astype(jnp.bfloat16), full_out).astype(jnp.bfloat16)
     grad_queries, pair_gradient_rows = attend_backward(

time: 945 us -> 557 us (0.59)
  the two profiles are of different devices: /device:TPU:2 before, /device:TPU:1 now
where the time goes in v1:
time: 557 us; the launch traced here: 556 us
  waiting for transfers between devices  371 us (67%)
  blocking collectives  50 us (9%)
  local copies, waits for them, and re-layouts  43.4 us (8%)
  matrix products  39.1 us (7%)
  starting transfers between devices  27.1 us (5%)
  between operations  14.1 us (3%)
  other arithmetic  11.4 us (2%)
    psum x1, waiting for transfers between devices, shards(): lax.psum(piece_in, shard_axis)  117 us
    all_gather x1, waiting for transfers between devices, shards(): full_out = lax.all_gather(out_weight, 'fsdp', axis=0, tiled=True)  87 us
    psum x1, waiting for transfers between devices, shards(): lax.psum(lax.psum(piece_in, shard_axis), axis_name)  61.3 us
    reduce_scatter x1, waiting for transfers between devices, shards(): lax.psum_scatter(head_term, 'fsdp', scatter_dimension=0, tiled=True)  52.7 us
    all_gather x1, blocking collectives, shards(): full_head = lax.all_gather(head_weight, 'fsdp', axis=0, tiled=True)  50 us
    all_gather x1, waiting for transfers between devices, shards(): lax.all_gather(query_key_value_weight, 'fsdp', axis=0, tiled=True)  49 us
    unnamed x58, local copies, waits for them, and re-layouts  12.2 us
    ppermute x2, starting transfers between devices, with_halo(): after = lax.ppermute(leading, axis, down)  11.8 us
  transfers between devices with their start and end apart: 11, of which 7 were waited for; matrix products, arithmetic and copies ran while one was open for 12% of the time, Pallas kernels for 0%

profile of v1, /device:TPU:1, one launch (start us, length us, event | category | flops | bytes accessed | tf_op | source)
XLA Modules:
  0.0 555.7 jit_solution(5916759297751713066)
XLA Ops:
  7.2 0.7 all-gather.3.cloned.1.call-update
  8.0 0.7 all-gather.5.cloned.1.call-update
  8.7 1.7 fusion.56
  10.4 3.9 collective-permute-start.2
  14.3 5.6 %collective-permute-start.3 = (f32[20,8,1]{2,1,0:T(8,128)}, f32[20,8,1]{2,1,0:T(8,128)}, u32[]{:S(2)}, u32[]{:S(2)}) collective-permute-start(f32[20,8,1]{2,1,0:T(8,128)} %get-tuple-element.12), channel_id=1, source_target_pairs={{1,0},{2,1},{3,2},{4,3},{5,4},{6,5},{7,6},{8,7},{9,8},{10,9},{11,1... | collective-permute-start | bytes 1928 | tf_op jit(solution)/shard_map/ppermute | solution.py:24
  20.0 1.3 convert_reduce_fusion
  22.4 1.5 copy.23
  23.9 1.1 convert_element_type.125
  25.0 0.6 broadcast_add_fusion
  25.6 50.0 %all_gather.11 = bf16[1536,320]{1,0:T(8,128)(2,1)S(1)} all-gather(bf16[96,320]{1,0:T(8,128)(2,1)} %param.11), channel_id=1, replica_groups=mesh['dp'=2,'fsdp'=16,'tile'=16] {'fsdp'}, dimensions={0}, use_global_device_ids=true | all-gather | bytes 1044480 | tf_op jit(solution)/shard_map/all_gather | solution.py:144
  75.6 1.6 fusion.59
  77.2 1.2 multiply_convert_fusion.1
  78.3 0.6 convert_multiply_fusion
  78.9 2.1 convolution_bitcast_fusion.1
  81.1 49.0 %all-gather.3.cloned.1.call-done = bf16[1536,2304]{1,0:T(8,128)(2,1)} async-done(((bf16[96,2304]{1,0:T(8,128)(2,1)}), bf16[1536,2304]{1,0:T(8,128)(2,1)}) %all-gather.3.cloned.1.call-update) | async-done | bytes 7077904 | tf_op jit(solution)/shard_map/all_gather | solution.py:132
  130.1 5.3 convolution_convert_fusion
  135.4 0.9 copy-done.9
  136.3 0.8 fusion.55
  137.1 2.5 collective-permute-start
  139.6 6.1 %collective-permute-start.1 = (bf16[8,8,1536]{2,1,0:T(8,128)(2,1)}, bf16[8,8,1536]{2,1,0:T(8,128)(2,1)}, u32[]{:S(2)}, u32[]{:S(2)}) collective-permute-start(bf16[8,8,1536]{2,1,0:T(8,128)(2,1)} %get-tuple-element.10), channel_id=1, source_target_pairs={{1,0},{2,1},{3,2},{4,3},{5,4},{6,5},{7,6},{8,7},{9,8},{10,9},{11,1... | collective-permute-start | bytes 589832 | tf_op jit(solution)/shard_map/ppermute | solution.py:24
  145.8 87.0 %all-gather.5.cloned.1.call-done = bf16[768,1536]{1,0:T(8,128)(2,1)} async-done(((bf16[48,1536]{1,0:T(8,128)(2,1)}), bf16[768,1536]{1,0:T(8,128)(2,1)}) %all-gather.5.cloned.1.call-update) | async-done | bytes 2359312 | tf_op jit(solution)/shard_map/all_gather | solution.py:141
  232.8 3.2 convolution_convert_fusion.1
  236.0 1.9 copy.24
  238.0 1.8 slice.50
  239.8 1.9 copy.18
  241.7 1.4 pad_maximum_fusion
  243.1 1.1 fusion.54
  244.2 2.1 copy.29
  246.3 2.2 copy.28
  248.5 4.0 fusion.57
  252.5 2.9 convolution_convert_fusion.2
  255.6 1.6 convolution_bitcast_fusion
  257.6 0.8 fusion.4
  258.4 0.9 copy-done.6
  259.3 2.1 fusion.60
  261.6 2.4 fusion.58
  264.0 2.4 reshape.187
  266.4 3.1 copy.20
  269.4 3.1 copy.21
  272.5 1.6 copy.26
  274.2 2.8 concatenate.20
  277.0 3.0 multiply_reduce_fusion
  280.0 0.7 multiply_convert_fusion
  280.7 1.1 copy-done.1
  282.3 1.7 copy.25
  284.0 1.9 concatenate.19
  286.0 1.1 copy-done.10
  287.3 1.5 copy-done.7
  288.7 0.9 fusion.53
  289.7 3.3 collective-permute-start.4
  293.0 5.3 collective-permute-start.5
  298.4 0.6 fusion.10
  299.0 1.0 copy.27
  300.0 2.2 fusion.11
  302.2 1.1 collective-permute-done.4
  303.3 1.1 collective-permute-done.5
  304.3 1.7 fusion.6
  306.1 6.9 %fusion.52 = (f32[256]{0:T(256)}, f32[256]{0:T(256)}, f32[256,1536]{1,0:T(8,128)}) fusion(f32[256]{0:T(256)S(1)} %rsqrt.12, f32[256]{0:T(256)S(1)} %div.51, bf16[1,8,32,1536]{3,2,1,0:T(8,128)(2,1)S(1)} %copy-done, f32[1536]{0:T(1024)S(1)} %copy-done.22, bf16[1536,2304]{1,0:T(8,128)(2,1)} %all-gather.3.cloned.1.call-done, ...), kind=kOutput, calls=%fused_computation.104 | convolution fusion | flops 1817050624 | bytes 10627072 | tf_op jit(solution)/shard_map/dot_general | solution.py:120
  313.0 52.7 %reduce-scatter.2.cloned.1.call-done = f32[96,320]{1,0:T(8,128)} async-done(((f32[1536,320]{1,0:T(8,128)}), f32[96,320]{1,0:T(8,128)}) %reduce-scatter.2.cloned.1.call-update) | async-done | bytes 122896 | tf_op jit(solution)/shard_map/reduce_scatter | solution.py:178
  365.7 0.7 broadcast_multiply_fusion.1
  366.4 117.0 %all-reduce.5.cloned.1.call-done = f32[96,320]{1,0:T(8,128)} async-done(((f32[96,320]{1,0:T(8,128)}), f32[96,320]{1,0:T(8,128)}) %all-reduce.5.cloned.1.call-update) | async-done | bytes 122896 | tf_op jit(solution)/shard_map/psum | solution.py:180
  483.4 2.9 add_convert_fusion
  486.3 61.3 %all-reduce.7.cloned.1.call-done = f32[96,320]{1,0:T(8,128)} async-done(((f32[96,320]{1,0:T(8,128)}), f32[96,320]{1,0:T(8,128)}) %all-reduce.7.cloned.1.call-update) | async-done | bytes 122896 | tf_op jit(solution)/shard_map/psum | solution.py:179
  547.6 1.6 copy.33
  (74 shorter events, 2.9 us)
Async XLA Ops:
  7.2 14.2 %copy-start = (bf16[1,8,32,1536]{3,2,1,0:T(8,128)(2,1)S(1)}, bf16[1,8,32,1536]{3,2,1,0:T(8,128)(2,1)}, u32[]{:S(2)}) copy-start(bf16[1,8,32,1536]{3,2,1,0:T(8,128)(2,1)} %param.7) | copy-start | bytes 2359300
  7.2 14.7 %copy-start.20 = (f32[1,20,32,128]{3,2,1,0:T(8,128)S(1)}, f32[1,20,32,128]{3,2,1,0:T(8,128)}, u32[]{:S(2)}) copy-start(f32[1,20,32,128]{3,2,1,0:T(8,128)} %param.13) | copy-start | bytes 983044
  7.2 122.9 %all-gather.3.cloned.1.call-start = ((), (), s32[]{:S(2)}) async-start(), calls=%async_computation.1 | async-start | bytes 7520256 | tf_op jit(solution)/shard_map/all_gather | solution.py:132
  7.9 224.9 %all-gather.5.cloned.1.call-start = ((), (), s32[]{:S(2)}) async-start(), calls=%async_computation.2 | async-start | bytes 2506752 | tf_op jit(solution)/shard_map/all_gather | solution.py:141
  8.7 357.0 %reduce-scatter.2.cloned.1.call-start = ((), (), s32[]{:S(2)}) async-start(), calls=%async_computation.3 | async-start | bytes 2506752 | tf_op jit(solution)/shard_map/reduce_scatter | solution.py:178
  10.4 68.5 %collective-permute-start.2 = (f32[20,8,1]{2,1,0:T(8,128)}, f32[20,8,1]{2,1,0:T(8,128)}, u32[]{:S(2)}, u32[]{:S(2)}) collective-permute-start(f32[20,8,1]{2,1,0:T(8,128)} %get-tuple-element.11), channel_id=1, source_target_pairs={{0,1},{1,2},{2,3},{3,4},{4,5},{5,6},{6,7},{7,8},{8,9},{9,10},{10,1... | collective-permute-start | bytes 1928 | tf_op jit(solution)/shard_map/ppermute | solution.py:23
  14.3 64.6 %collective-permute-start.3 = (f32[20,8,1]{2,1,0:T(8,128)}, f32[20,8,1]{2,1,0:T(8,128)}, u32[]{:S(2)}, u32[]{:S(2)}) collective-permute-start(f32[20,8,1]{2,1,0:T(8,128)} %get-tuple-element.12), channel_id=1, source_target_pairs={{1,0},{2,1},{3,2},{4,3},{5,4},{6,5},{7,6},{8,7},{9,8},{10,9},{11,1... | collective-permute-start | bytes 1928 | tf_op jit(solution)/shard_map/ppermute | solution.py:24
  75.6 1.6 copy-start.21
  75.6 3.4 copy-start.15
  135.3 1.8 copy-start.13
  135.4 0.9 copy-start.9
  137.1 104.6 %collective-permute-start = (bf16[8,8,1536]{2,1,0:T(8,128)(2,1)}, bf16[8,8,1536]{2,1,0:T(8,128)(2,1)}, u32[]{:S(2)}, u32[]{:S(2)}) collective-permute-start(bf16[8,8,1536]{2,1,0:T(8,128)(2,1)} %get-tuple-element.9), channel_id=1, source_target_pairs={{0,1},{1,2},{2,3},{3,4},{4,5},{5,6},{6,7},{7,8},{8,9},{9,10},{10,1... | collective-permute-start | bytes 589832 | tf_op jit(solution)/shard_map/ppermute | solution.py:23
  139.6 102.1 %collective-permute-start.1 = (bf16[8,8,1536]{2,1,0:T(8,128)(2,1)}, bf16[8,8,1536]{2,1,0:T(8,128)(2,1)}, u32[]{:S(2)}, u32[]{:S(2)}) collective-permute-start(bf16[8,8,1536]{2,1,0:T(8,128)(2,1)} %get-tuple-element.10), channel_id=1, source_target_pairs={{1,0},{2,1},{3,2},{4,3},{5,4},{6,5},{7,6},{8,7},{9,8},{10,9},{11,1... | collective-permute-start | bytes 589832 | tf_op jit(solution)/shard_map/ppermute | solution.py:24
  252.5 3.0 copy-start.3
  252.5 3.1 copy-start.17
  255.6 2.0 copy-start.5
  257.6 1.7 copy-start.12
  258.4 0.9 copy-start.6
  261.3 222.1 %all-reduce.5.cloned.1.call-start = ((), (), s32[]{:S(2)}) async-start(), calls=%async_computation.4 | async-start | bytes 294912 | tf_op jit(solution)/shard_map/psum | solution.py:180
  269.4 3.1 copy-start.14
  274.2 2.8 copy-start.16
  274.2 2.8 copy-start.18
  277.0 3.0 copy-start.4
  279.9 1.9 copy-start.11
  280.7 1.2 copy-start.1
  285.8 1.3 copy-start.10
  287.1 11.2 %copy-start.2 = (bf16[8,256,384]{2,1,0:T(8,128)(2,1)S(1)}, bf16[8,256,384]{2,1,0:T(8,128)(2,1)}, u32[]{:S(2)}) copy-start(bf16[8,256,384]{2,1,0:T(8,128)(2,1)} %copy-done.1) | copy-start | bytes 4718596
  287.1 11.3 %copy-start.8 = (bf16[384,768]{0,1:T(8,128)(2,1)S(1)}, bf16[384,768]{0,1:T(8,128)(2,1)}, u32[]{:S(2)}) copy-start(bf16[384,768]{0,1:T(8,128)(2,1)} %copy.29) | copy-start | bytes 1769476
  287.3 1.5 copy-start.7
  289.7 13.6 %collective-permute-start.4 = (f32[8,8,1536]{2,1,0:T(8,128)}, f32[8,8,1536]{2,1,0:T(8,128)}, u32[]{:S(2)}, u32[]{:S(2)}) collective-permute-start(f32[8,8,1536]{2,1,0:T(8,128)} %get-tuple-element.5), channel_id=1, source_target_pairs={{0,1},{1,2},{2,3},{3,4},{4,5},{5,6},{6,7},{7,8},{8,9},{9,10},{10,1... | collective-permute-start | bytes 1179656 | tf_op jit(solution)/shard_map/ppermute | solution.py:32
  293.0 7.0 %copy-start.23 = (s32[128]{0:T(128)S(1)}, s32[128]{0:T(128)}, u32[]{:S(2)}) copy-start(s32[128]{0:T(128)} %get-tuple-element.24) | copy-start | bytes 1540
  293.0 7.0 %copy-start.24 = (s32[128]{0:T(128)S(1)}, s32[128]{0:T(128)}, u32[]{:S(2)}) copy-start(s32[128]{0:T(128)} %get-tuple-element.25) | copy-start | bytes 1540
  293.0 7.0 %copy-start.25 = (f32[128]{0:T(128)S(1)}, f32[128]{0:T(128)}, u32[]{:S(2)}) copy-start(f32[128]{0:T(128)} %get-tuple-element.22) | copy-start | bytes 1540
  293.0 7.0 %copy-start.26 = (f32[128]{0:T(128)S(1)}, f32[128]{0:T(128)}, u32[]{:S(2)}) copy-start(f32[128]{0:T(128)} %get-tuple-element.23) | copy-start | bytes 1540
  293.0 11.3 %collective-permute-start.5 = (f32[8,8,1536]{2,1,0:T(8,128)}, f32[8,8,1536]{2,1,0:T(8,128)}, u32[]{:S(2)}, u32[]{:S(2)}) collective-permute-start(f32[8,8,1536]{2,1,0:T(8,128)} %get-tuple-element.6), channel_id=1, source_target_pairs={{0,15},{1,0},{2,1},{3,2},{4,3},{5,4},{6,5},{7,6},{8,7},{9,8},{10,9... | collective-permute-start | bytes 1179656 | tf_op jit(solution)/shard_map/ppermute | solution.py:32
  302.2 3.8 copy-start.19
  302.2 3.9 copy-start.22
  365.7 181.9 %all-reduce.7.cloned.1.call-start = ((), (), s32[]{:S(2)}) async-start(), calls=%async_computation.5 | async-start | bytes 294912 | tf_op jit(solution)/shard_map/psum | solution.py:179
Sparse Core Ops, SparseCore 0:
  10.1 119.9 all-gather.2
  132.1 100.6 all-gather.4
  261.5 104.1 reduce-scatter.1
  368.7 114.6 all-reduce.4
  486.1 61.4 all-reduce.6
